TPU v7x, 128 devices: a whole 4x4x4 slice. The times are simulated.
128 devices in a mesh: dp: 32 (over z, x, core), mp: 4 (over y).
Axes of the slice: x: 4, y: 4, z: 4, core: 2. Of those that a mesh axis runs over, the one named last changes fastest.
Arguments:
- hidden: bfloat16 [40960, 8192], P('dp', 'mp'), may hold values from -6 to 6
- rewards: float32 [256, 160], P('dp'), may hold values from -4 to 4
- lengths: int32 [256], P('dp'), may hold values from 1 to 160, as said below
- dest_shard: int32 [256], P('dp'), may hold values from 0 to 31, as said below
- source_owner: int32 [256], P('dp'), may hold values from 0 to 31, as said below
- pack_offset: int32 [256], P('dp'), may hold values from 0 to 639, as said below
- segment_ids: int32 [20480], P('dp'), may hold values from 0 to 7, as said below
- norm_gain: float32 [8192], replicated, may hold values from 0.5 to 1.5
- w_query: bfloat16 [8192, 4096], P(None, 'mp'), may hold values from -1 to 1
- w_key: bfloat16 [8192, 512], P(None, 'mp'), may hold values from -1 to 1
- w_value: bfloat16 [8192, 512], P(None, 'mp'), may hold values from -0.0625 to 0.0625
- value_head: float32 [8192], P('mp'), may hold values from -0.0625 to 0.0625
- folded_head: float32 [4096], P('mp'), may hold values from -0.09375 to 0.09375
Outputs:
- values: float32 [256, 160], P('dp')
- advantages: float32 [256, 160], P('dp')
Inputs may be any that keep to these rules, and one draw needn't show every extreme that they name: `lengths`: rows of a slot past its rollout's length are unused. Every critic shard holds a rollout of 160 rows. Some owner's 8 rollouts all have 160 rows. `dest_shard`: owner o packs its 8 rollouts on the shards o, o + 1, ..., o + 7, modulo the number of shards, one on each. `source_owner`: shard s packs one rollout from each of the owners s, s - 1, ..., s - 7, modulo the number of shards, in some order, agreeing with dest_shard. `pack_offset`: A shard's packed rollouts lie back to back in the order of their index, each with the length that lengths gives it, and fill all 640 rows. `segment_ids`: each packed row names the index of the packed rollout that holds it, as pack_offset and lengths lay them out.
All inputs are finite; a program needn't handle non-finite values.
Results may differ from a plain program's by a relative error of at most 0.007.
Values may be sent and summed in bfloat16 or wider, within the bound.
A program may use at most 192 MiB of HBM per device.

v0:
```python
import math
import jax
import jax.numpy as jnp
from jax import lax
from jax.sharding import PartitionSpec as P

HD = 128
EPSILON = 1e-05
DISCOUNT = 0.99
SMOOTHING = 0.95
ROPE_BASE = 500000.0


def passed_along(value, axis, by):
    length = lax.axis_size(axis)
    return lax.ppermute(value, axis, [(i, (i + by) % length) for i in range(length)])


def rotary(values_in, positions):
    half_width = values_in.shape[-1] // 2
    frequency = ROPE_BASE ** (-jnp.arange(half_width, dtype=jnp.float32) / half_width)
    angles = positions.astype(jnp.float32)[:, None] * frequency[None, :]
    cosine = jnp.cos(angles)[:, None, :]
    sine_part = jnp.sin(angles)[:, None, :]
    front_half = values_in[..., :half_width]
    back_half = values_in[..., half_width:]
    return jnp.concatenate(
        [front_half * cosine - back_half * sine_part, back_half * cosine + front_half * sine_part],
        axis=-1,
    )


def head_values(queries, keys_out, values_out, segments, positions, folded_head):
    row_count = queries.shape[0]
    kv_count = keys_out.shape[1] // HD
    group_size = queries.shape[1] // HD // kv_count
    query_rot = rotary(queries.reshape(row_count, kv_count * group_size, HD), positions).astype(
        jnp.bfloat16
    )
    query_rot = query_rot.reshape(row_count, kv_count, group_size, HD)
    key_rot = rotary(keys_out.reshape(row_count, kv_count, HD), positions).astype(jnp.bfloat16)
    value_rows = values_out.astype(jnp.bfloat16).reshape(row_count, kv_count, HD)
    scores = jnp.einsum(
        "qhgd,khd->hgqk", query_rot, key_rot, preferred_element_type=jnp.float32
    ) / math.sqrt(HD)
    allowed = (segments[:, None] == segments[None, :]) & (positions[:, None] >= positions[None, :])
    scores = jnp.where(allowed[None, None], scores, -1e30)
    row_max = jnp.max(scores, axis=-1, keepdims=True)
    exp_scores = jnp.where(allowed[None, None], jnp.exp(scores - row_max), 0.0)
    row_total = jnp.sum(exp_scores, axis=-1, keepdims=True)
    weights = (exp_scores / row_total).astype(jnp.bfloat16)
    attended = jnp.einsum("hgqk,khd->qhgd", weights, value_rows, preferred_element_type=jnp.float32)
    return jnp.sum(attended.reshape(row_count, -1) * folded_head[None, :], axis=1)


def local(
    hidden,
    rewards,
    lengths,
    dest_shard,
    source_owner,
    pack_offset,
    segment_ids,
    norm_gain,
    w_query,
    w_key,
    w_value,
    value_head,
    folded_head,
):
    shards = lax.axis_size("dp")
    shard_index = lax.axis_index("dp")
    rollouts = lengths.shape[0]
    slot_rows = rewards.shape[1]
    packed_rows = segment_ids.shape[0]
    slot_lanes = jnp.arange(rollouts, dtype=jnp.int32)

    def slot_for(shift_by):
        target = (shard_index + shift_by) % shards
        return jnp.sum(jnp.where(dest_shard == target, slot_lanes, 0))

    def outgoing(shift_by, source):
        return lax.dynamic_slice_in_dim(source, slot_for(shift_by) * slot_rows, slot_rows, 0)

    source_step = (shard_index - source_owner) % shards
    lane_match = segment_ids[:, None] == slot_lanes[None, :]
    row_step = jnp.sum(jnp.where(lane_match, source_step[None, :], 0), axis=1)
    row_offset = jnp.sum(jnp.where(lane_match, pack_offset[None, :], 0), axis=1)
    positions = jnp.arange(packed_rows, dtype=jnp.int32) - row_offset
    pick_rows = row_step * slot_rows + positions
    received = [outgoing(0, hidden)]
    for shift_by in range(1, rollouts):
        received.append(passed_along(outgoing(shift_by, hidden), "dp", shift_by))
    own_part = jnp.take(jnp.concatenate(received, axis=0), pick_rows, axis=0)
    packed = lax.all_gather(own_part, "mp", axis=1, tiled=True)
    packed_f = packed.astype(jnp.float32)
    row_scale = lax.rsqrt(jnp.mean(packed_f * packed_f, axis=1) + EPSILON)
    normed = (packed_f * row_scale[:, None] * norm_gain[None, :]).astype(jnp.bfloat16)
    queries = jnp.dot(normed, w_query, preferred_element_type=jnp.float32)
    keys_out = jnp.dot(normed, w_key, preferred_element_type=jnp.float32)
    values_out = jnp.dot(normed, w_value, preferred_element_type=jnp.float32)
    value_terms = head_values(queries, keys_out, values_out, segment_ids, positions, folded_head)
    value_terms = value_terms + jnp.sum(own_part.astype(jnp.float32) * value_head[None, :], axis=1)
    packed_values = lax.psum(value_terms, "mp")
    padded = jnp.concatenate([packed_values, jnp.zeros((slot_rows,), jnp.float32)])
    slot_values = jnp.zeros((rollouts, slot_rows), jnp.float32)
    for shift_by in range(rollouts):
        owner_now = (shard_index - shift_by) % shards
        j_index = jnp.sum(jnp.where(source_owner == owner_now, slot_lanes, 0))
        start_at = jnp.sum(jnp.where(slot_lanes == j_index, pack_offset, 0))
        arrived = lax.dynamic_slice_in_dim(padded, start_at, slot_rows, 0)
        if shift_by:
            arrived = passed_along(arrived, "dp", -shift_by)
        slot_values = jnp.where(
            (slot_lanes == slot_for(shift_by))[:, None], arrived[None, :], slot_values
        )
    step_ids = jnp.arange(slot_rows, dtype=jnp.int32)
    live_mask = step_ids[None, :] < lengths[:, None]
    values = jnp.where(live_mask, slot_values, 0.0)
    next_live = step_ids[None, :] + 1 < lengths[:, None]
    following = jnp.concatenate([values[:, 1:], jnp.zeros((rollouts, 1), jnp.float32)], axis=1)
    one_step = jnp.where(
        live_mask, rewards + DISCOUNT * jnp.where(next_live, following, 0.0) - values, 0.0
    )
    lag_matrix = (step_ids[:, None] - step_ids[None, :]).astype(jnp.float32)
    decay_table = jnp.where(
        lag_matrix >= 0, jnp.exp(lag_matrix * math.log(DISCOUNT * SMOOTHING)), 0.0
    )
    advantages = jnp.dot(one_step, decay_table, precision=lax.Precision.HIGHEST)
    return (values, advantages)


def solution(mesh):
    return jax.shard_map(
        local,
        mesh=mesh,
        in_specs=(
            P("dp", "mp"),
            P("dp", None),
            P("dp"),
            P("dp"),
            P("dp"),
            P("dp"),
            P("dp"),
            P(),
            P(None, "mp"),
            P(None, "mp"),
            P(None, "mp"),
            P("mp"),
            P("mp"),
        ),
        out_specs=(P("dp", None), P("dp", None)),
        check_vma=False,
    )
```

profile of v0, /device:TPU:1, one launch (start us, length us, event | category | flops | bytes accessed | tf_op | source)
XLA Modules:
  0.0 324.4 jit_solution(14331908132062440243)
XLA Ops:
  7.4 1.9 fusion.49
  14.4 3.8 %constant_dynamic-slice_fusion = (bf16[160,2048]{1,0:T(8,128)(2,1)S(1)}, bf16[160,2048]{1,0:T(8,128)(2,1)S(1)}, bf16[160,2048]{1,0:T(8,128)(2,1)S(1)}, bf16[160,...) fusion(bf16[1280,2048]{1,0:T(8,128)(2,1)} %param.13, ...), kind=kLoop, calls=%fused_computation.98 | loop fusion | bytes 10485792 | tf_op jit(solution)/shard_map/dynamic_slice | solution.py:83
  18.2 2.6 collective-permute-start
  20.8 1.2 collective-permute-start.1
  22.0 1.5 collective-permute-start.2
  23.5 1.9 collective-permute-start.3
  25.4 3.4 %collective-permute-start.4 = (bf16[160,2048]{1,0:T(8,128)(2,1)S(1)}, bf16[160,2048]{1,0:T(8,128)(2,1)S(1)}, u32[]{:S(2)}, u32[]{:S(2)}) collective-permute-start(bf16[160,2048]{1,0:T(8,128)(2,1)S(1)} %get-tuple-element.33), channel_id=1, source_target_pairs={{0,20},{4,24},{8,28},{12,32},{16,36},{20,40},{24,44},{28,48},{32,5... | collective-permute-start | bytes 1966088 | tf_op jit(solution)/shard_map/ppermute | solution.py:16
  28.9 5.8 %collective-permute-done = bf16[160,2048]{1,0:T(8,128)(2,1)S(1)} collective-permute-done((bf16[160,2048]{1,0:T(8,128)(2,1)S(1)}, bf16[160,2048]{1,0:T(8,128)(2,1)S(1)}, u32[]{:S(2)}, u32[]{:S(2)}) %collective-permute-start) | collective-permute-done | bytes 655392 | tf_op jit(solution)/shard_map/ppermute | solution.py:16
  34.8 2.8 collective-permute-start.5
  37.6 0.9 constant_dynamic-update-slice_fusion.6
  38.5 14.7 %collective-permute-done.1 = bf16[160,2048]{1,0:T(8,128)(2,1)S(1)} collective-permute-done((bf16[160,2048]{1,0:T(8,128)(2,1)S(1)}, bf16[160,2048]{1,0:T(8,128)(2,1)S(1)}, u32[]{:S(2)}, u32[]{:S(2)}) %collective-permute-start.1) | collective-permute-done | bytes 655392 | tf_op jit(solution)/shard_map/ppermute | solution.py:16
  53.1 0.9 constant_dynamic-update-slice_fusion.5
  54.1 8.8 %collective-permute-done.2 = bf16[160,2048]{1,0:T(8,128)(2,1)S(1)} collective-permute-done((bf16[160,2048]{1,0:T(8,128)(2,1)S(1)}, bf16[160,2048]{1,0:T(8,128)(2,1)S(1)}, u32[]{:S(2)}, u32[]{:S(2)}) %collective-permute-start.2) | collective-permute-done | bytes 655392 | tf_op jit(solution)/shard_map/ppermute | solution.py:16
  62.8 0.9 constant_dynamic-update-slice_fusion.4
  63.8 35.7 %collective-permute-done.3 = bf16[160,2048]{1,0:T(8,128)(2,1)S(1)} collective-permute-done((bf16[160,2048]{1,0:T(8,128)(2,1)S(1)}, bf16[160,2048]{1,0:T(8,128)(2,1)S(1)}, u32[]{:S(2)}, u32[]{:S(2)}) %collective-permute-start.3) | collective-permute-done | bytes 655392 | tf_op jit(solution)/shard_map/ppermute | solution.py:16
  99.4 0.9 constant_dynamic-update-slice_fusion.3
  100.4 0.9 constant_dynamic-update-slice_fusion.2
  101.3 7.6 %collective-permute-done.5 = bf16[160,2048]{1,0:T(8,128)(2,1)S(1)} collective-permute-done((bf16[160,2048]{1,0:T(8,128)(2,1)S(1)}, bf16[160,2048]{1,0:T(8,128)(2,1)S(1)}, u32[]{:S(2)}, u32[]{:S(2)}) %collective-permute-start.5) | collective-permute-done | bytes 655392 | tf_op jit(solution)/shard_map/ppermute | solution.py:16
  108.9 0.9 constant_dynamic-update-slice_fusion.1
  109.8 5.4 %collective-permute-done.6 = bf16[160,2048]{1,0:T(8,128)(2,1)S(1)} collective-permute-done((bf16[160,2048]{1,0:T(8,128)(2,1)S(1)}, bf16[160,2048]{1,0:T(8,128)(2,1)S(1)}, u32[]{:S(2)}, u32[]{:S(2)}) %collective-permute-start.6) | collective-permute-done | bytes 655392 | tf_op jit(solution)/shard_map/ppermute | solution.py:16
  115.1 0.9 constant_dynamic-update-slice_fusion
  116.0 10.1 %gather_fusion = bf16[640,2048]{1,0:T(8,128)(2,1)} fusion(bf16[1280,2048]{1,0:T(8,128)(2,1)} %constant_dynamic-update-slice_fusion, s32[1024]{0:T(1024)S(1)} %pad_clamp_fusion), kind=kCustom, calls=%fused_computation | custom fusion | bytes 5245440 | tf_op jit(solution)/shard_map/jit(_take)/gather | solution.py:94
  126.1 4.1 %multiply_reduce_fusion = (f32[640]{0:T(1024)S(1)}, bf16[640,2048]{1,0:T(8,128)(2,1)}) fusion(f32[2048]{0:T(1024)S(1)} %copy-done.6, bf16[640,2048]{1,0:T(8,128)(2,1)} %gather_fusion, pred[640]{0:T(1024)(128)(4,1)S(1)} %compare_and_fusion.1), kind=kLoop, calls=%fused_computation.13 | loop fusion | flops 5242240 | bytes 5254272 | tf_op jit(solution)/shard_map/reduce_sum | solution.py:103
  130.2 5.9 %fusion.58 = (s32[]{:T(128)}, s32[]{:T(128)}, s32[]{:T(128)}, s32[]{:T(128)}, s32[]{:T(128)}, /*index=5*/s32[]{:T(128)}, s32[]{:T(128)}, s32[]{:T(128)}) fusion(s32[8]{0:T(128)S(1)} %copy-done.7, s32[]{:T(128)} %get-tuple-element.67, s32[]{:T(128)} %get-tuple-element.66, s32[]{:T(128)} %get-tuple-element.65, s32[]{:T(128)} %get-tuple-element.64, ...), kind=kLoop, calls=%fused_computation.140 | loop fusion | flops 184 | bytes 96 | tf_op jit(solution)/shard_map/reduce_sum | solution.py:110
  151.1 1.3 iota_compare_fusion.3
  152.4 1.2 iota_compare_fusion.4
  153.6 1.1 iota_compare_fusion.5
  154.7 1.2 iota_compare_fusion.6
  155.9 1.2 iota_compare_fusion.7
  157.0 1.2 iota_compare_fusion.8
  158.8 1.1 compare_and_fusion
  159.9 2.0 multiply_cosine_fusion
  161.9 69.3 %all-gather.2.cloned.1.call-done = bf16[640,8192]{1,0:T(8,128)(2,1)} async-done(((bf16[640,2048]{1,0:T(8,128)(2,1)}), bf16[640,8192]{1,0:T(8,128)(2,1)}) %all-gather.2.cloned.1.call-update) | async-done | bytes 10485776 | tf_op jit(solution)/shard_map/all_gather | solution.py:95
  231.2 6.2 %fusion = f32[640]{0:T(1024)S(1)} fusion(bf16[640,8192]{1,0:T(8,128)(2,1)} %all-gather.2.cloned.1.call-done), kind=kLoop, calls=%fused_computation.3 | loop fusion | flops 15728000 | bytes 10488320 | tf_op jit(solution)/shard_map/reduce_sum | solution.py:97
  238.2 14.8 %convolution_bitcast_fusion = f32[80,8,8,128]{3,1,2,0:T(8,128)S(1)} fusion(bf16[8192,1024]{1,0:T(8,128)(2,1)} %param.21, bf16[640,8192]{1,0:T(8,128)(2,1)S(1)} %copy-done.2, f32[8192]{0:T(1024)} %param.20, f32[640]{0:T(1024)S(1)} %add_rsqrt_fusion), kind=kOutput, calls=%fused_computation.19 | convolution fusion | flops 10758389760 | bytes 29919744 | tf_op jit(solution)/shard_map/dot_general | solution.py:99
  254.5 4.9 %convolution_bitcast_fusion.1 = f32[640,1,128]{0,2,1:T(8,128)} fusion(bf16[8192,128]{1,0:T(8,128)(2,1)S(1)} %copy-done, bf16[640,8192]{1,0:T(8,128)(2,1)S(1)} %copy-done.2, f32[8192]{0:T(1024)} %param.20, f32[640]{0:T(1024)S(1)} %add_rsqrt_fusion), kind=kOutput, calls=%fused_computation.25 | convolution fusion | flops 1363148800 | bytes 12945920 | tf_op jit(solution)/shard_map/dot_general | solution.py:100
  259.3 1.7 fusion.36
  261.1 2.1 subtract_convert_fusion
  263.2 6.4 %fusion.3 = (f32[8,640]{1,0:T(8,128)S(1)}, f32[640,640,8]{1,0,2:T(8,128)}) fusion(pred[640,640]{0,1:T(8,128)(4,1)S(1)} %copy-done.3, bf16[640,8,64]{2,0,1:T(8,128)(2,1)S(1)} %get-tuple-element.31, bf16[640,8,64]{2,0,1:T(8,128)(2,1)S(1)} %get-tuple-element.30, bf16[640,64]{0,1:T(8,128)(2,1)S(1)} %get-tuple-element.43, bf16[640,64]{0,1:T(8,128)(2,1)S(1)} %get-tuple-element.42), kind=kOutput, calls=%fused_computation.9 | convolution fusion | flops 851635200 | bytes 15011840 | tf_op jit(solution)/shard_map/qhgd,khd->hgqk/dot_general | solution.py:43
  269.6 7.8 %fusion.4 = f32[8,640]{1,0:T(8,128)S(1)} fusion(f32[640,640,8]{1,0,2:T(8,128)} %get-tuple-element.58, f32[8,640]{1,0:T(8,128)S(1)} %get-tuple-element.57, pred[640,640]{0,1:T(8,128)(4,1)S(1)} %copy-done.3), kind=kLoop, calls=%fused_computation.10 | loop fusion | flops 16378880 | bytes 13557760 | tf_op jit(solution)/shard_map/reduce_sum | solution.py:50
  277.5 14.9 %fusion.7 = f32[640]{0:T(1024)S(1)} fusion(f32[8,640]{1,0:T(8,128)S(1)} %fusion.4, f32[8,640]{1,0:T(8,128)S(1)} %get-tuple-element.57, f32[640,640,8]{1,0,2:T(8,128)} %get-tuple-element.58, pred[640,640]{0,1:T(8,128)(4,1)S(1)} %copy-done.3, f32[8,128]{1,0:T(8,128)S(1)} %bitcast.51, bf16[8192,128]{1,0:T(8,128)(2,1)} %param.23, ...), kind=kOutput, calls=%fused_computation.15 | convolution fusion | flops 2223062528 | bytes 26182656 | tf_op jit(solution)/shard_map/hgqk,khd->qhgd/dot_general | solution.py:52
  292.4 7.2 %psum.7 = f32[640]{0:T(1024)S(1)} all-reduce(f32[640]{0:T(1024)S(1)} %add.252), channel_id=1, replica_groups=mesh['dp'=32,'mp'=4] {'mp'}, use_global_device_ids=true, to_apply=%region_15.16 | all-reduce | flops 640 | bytes 5120 | tf_op jit(solution)/shard_map/psum | solution.py:104
  299.8 3.0 collective-permute-start.13
  302.7 5.0 %collective-permute-start.12 = (f32[160]{0:T(256)S(1)}, f32[160]{0:T(256)S(1)}, u32[]{:S(2)}, u32[]{:S(2)}) collective-permute-start(f32[160]{0:T(256)S(1)} %get-tuple-element.51), channel_id=1, source_target_pairs={{0,120},{4,124},{8,0},{12,4},{16,8},{20,12},{24,16},{28,20},{32,24... | collective-permute-start | bytes 1928 | tf_op jit(solution)/shard_map/ppermute | solution.py:16
  308.3 0.9 collective-permute-start.11
  309.5 3.1 collective-permute-start.9
  314.6 1.7 collective-permute-done.8
  316.7 0.8 fusion.25
  (70 shorter events, 6.3 us)
Async XLA Ops:
  7.2 247.3 %copy-start = (bf16[8192,128]{1,0:T(8,128)(2,1)S(1)}, bf16[8192,128]{1,0:T(8,128)(2,1)}, u32[]{:S(2)}) copy-start(bf16[8192,128]{1,0:T(8,128)(2,1)} %param.22) | copy-start | bytes 6291460
  7.2 224.0 %all-gather.2.cloned.1.call-start = ((), (), s32[]{:S(2)}) async-start(), calls=%async_computation | async-start | bytes 13107200 | tf_op jit(solution)/shard_map/all_gather | solution.py:95
  14.4 14.4 %copy-start.4 = (s32[640]{0:T(1024)S(1)}, s32[640]{0:T(1024)}, u32[]{:S(2)}) copy-start(s32[640]{0:T(1024)} %param.19) | copy-start | bytes 7684
  14.4 14.4 %copy-start.7 = (s32[8]{0:T(128)S(1)}, s32[8]{0:T(128)}, u32[]{:S(2)}) copy-start(s32[8]{0:T(128)} %param.18) | copy-start | bytes 100
  18.2 16.6 %collective-permute-start = (bf16[160,2048]{1,0:T(8,128)(2,1)S(1)}, bf16[160,2048]{1,0:T(8,128)(2,1)S(1)}, u32[]{:S(2)}, u32[]{:S(2)}) collective-permute-start(bf16[160,2048]{1,0:T(8,128)(2,1)S(1)} %get-tuple-element.37), channel_id=1, source_target_pairs={{0,4},{4,8},{8,12},{12,16},{16,20},{20,24},{24,28},{28,32},{32,36}... | collective-permute-start | bytes 1966088 | tf_op jit(solution)/shard_map/ppermute | solution.py:16
  20.8 32.4 %collective-permute-start.1 = (bf16[160,2048]{1,0:T(8,128)(2,1)S(1)}, bf16[160,2048]{1,0:T(8,128)(2,1)S(1)}, u32[]{:S(2)}, u32[]{:S(2)}) collective-permute-start(bf16[160,2048]{1,0:T(8,128)(2,1)S(1)} %get-tuple-element.36), channel_id=1, source_target_pairs={{0,8},{4,12},{8,16},{12,20},{16,24},{20,28},{24,32},{28,36},{32,40... | collective-permute-start | bytes 1966088 | tf_op jit(solution)/shard_map/ppermute | solution.py:16
  22.0 40.8 %collective-permute-start.2 = (bf16[160,2048]{1,0:T(8,128)(2,1)S(1)}, bf16[160,2048]{1,0:T(8,128)(2,1)S(1)}, u32[]{:S(2)}, u32[]{:S(2)}) collective-permute-start(bf16[160,2048]{1,0:T(8,128)(2,1)S(1)} %get-tuple-element.35), channel_id=1, source_target_pairs={{0,12},{4,16},{8,20},{12,24},{16,28},{20,32},{24,36},{28,40},{32,4... | collective-permute-start | bytes 1966088 | tf_op jit(solution)/shard_map/ppermute | solution.py:16
  23.5 75.9 %collective-permute-start.3 = (bf16[160,2048]{1,0:T(8,128)(2,1)S(1)}, bf16[160,2048]{1,0:T(8,128)(2,1)S(1)}, u32[]{:S(2)}, u32[]{:S(2)}) collective-permute-start(bf16[160,2048]{1,0:T(8,128)(2,1)S(1)} %get-tuple-element.34), channel_id=1, source_target_pairs={{0,16},{4,20},{8,24},{12,28},{16,32},{20,36},{24,40},{28,44},{32,4... | collective-permute-start | bytes 1966088 | tf_op jit(solution)/shard_map/ppermute | solution.py:16
  25.4 75.0 %collective-permute-start.4 = (bf16[160,2048]{1,0:T(8,128)(2,1)S(1)}, bf16[160,2048]{1,0:T(8,128)(2,1)S(1)}, u32[]{:S(2)}, u32[]{:S(2)}) collective-permute-start(bf16[160,2048]{1,0:T(8,128)(2,1)S(1)} %get-tuple-element.33), channel_id=1, source_target_pairs={{0,20},{4,24},{8,28},{12,32},{16,36},{20,40},{24,44},{28,48},{32,5... | collective-permute-start | bytes 1966088 | tf_op jit(solution)/shard_map/ppermute | solution.py:16
  34.8 74.1 %collective-permute-start.5 = (bf16[160,2048]{1,0:T(8,128)(2,1)S(1)}, bf16[160,2048]{1,0:T(8,128)(2,1)S(1)}, u32[]{:S(2)}, u32[]{:S(2)}) collective-permute-start(bf16[160,2048]{1,0:T(8,128)(2,1)S(1)} %get-tuple-element.39), channel_id=1, source_target_pairs={{0,24},{4,28},{8,32},{12,36},{16,40},{20,44},{24,48},{28,52},{32,5... | collective-permute-start | bytes 1966088 | tf_op jit(solution)/shard_map/ppermute | solution.py:16
  53.1 62.0 %collective-permute-start.6 = (bf16[160,2048]{1,0:T(8,128)(2,1)S(1)}, bf16[160,2048]{1,0:T(8,128)(2,1)S(1)}, u32[]{:S(2)}, u32[]{:S(2)}) collective-permute-start(bf16[160,2048]{1,0:T(8,128)(2,1)S(1)} %get-tuple-element.32), channel_id=1, source_target_pairs={{0,28},{4,32},{8,36},{12,40},{16,44},{20,48},{24,52},{28,56},{32,6... | collective-permute-start | bytes 1966088 | tf_op jit(solution)/shard_map/ppermute | solution.py:16
  116.0 10.1 %copy-start.6 = (f32[2048]{0:T(1024)S(1)}, f32[2048]{0:T(1024)}, u32[]{:S(2)}) copy-start(f32[2048]{0:T(1024)} %param.24) | copy-start | bytes 24580
  151.1 10.8 %copy-start.8 = (f32[64]{0:T(128)}, f32[64]{0:T(128)S(1)}, u32[]{:S(2)}) copy-start(f32[64]{0:T(128)S(1)} %multiply_power_fusion) | copy-start | bytes 772
  231.2 7.0 %copy-start.2 = (bf16[640,8192]{1,0:T(8,128)(2,1)S(1)}, bf16[640,8192]{1,0:T(8,128)(2,1)}, u32[]{:S(2)}) copy-start(bf16[640,8192]{1,0:T(8,128)(2,1)} %all-gather.2.cloned.1.call-done) | copy-start | bytes 31457284
  259.3 3.8 %copy-start.3 = (pred[640,640]{0,1:T(8,128)(4,1)S(1)}, pred[640,640]{0,1:T(8,128)(4,1)}, u32[]{:S(2)}) copy-start(pred[640,640]{0,1:T(8,128)(4,1)} %compare_and_fusion) | copy-start | bytes 1228804
  269.6 7.8 %copy-start.16 = (f32[8192]{0:T(1024)S(1)}, f32[8192]{0:T(1024)}, u32[]{:S(2)}) copy-start(f32[8192]{0:T(1024)} %param.20) | copy-start | bytes 98308
  269.6 7.8 %copy-start.18 = (f32[1024]{0:T(1024)S(1)}, f32[1024]{0:T(1024)}, u32[]{:S(2)}) copy-start(f32[1024]{0:T(1024)} %param.25) | copy-start | bytes 12292
  277.4 39.0 %copy-start.9 = (s32[8]{0:T(128)S(1)}, s32[8]{0:T(128)}, u32[]{:S(2)}) copy-start(s32[8]{0:T(128)} %param.15) | copy-start | bytes 100
  277.4 39.0 %copy-start.10 = (pred[8]{0:T(512)(128)(4,1)S(1)}, pred[8]{0:T(512)(128)(4,1)}, u32[]{:S(2)}) copy-start(pred[8]{0:T(512)(128)(4,1)} %iota_compare_fusion.3) | copy-start | bytes 28
  277.5 39.0 %copy-start.11 = (pred[8]{0:T(512)(128)(4,1)S(1)}, pred[8]{0:T(512)(128)(4,1)}, u32[]{:S(2)}) copy-start(pred[8]{0:T(512)(128)(4,1)} %iota_compare_fusion.4) | copy-start | bytes 28
  277.5 39.0 %copy-start.12 = (pred[8]{0:T(512)(128)(4,1)S(1)}, pred[8]{0:T(512)(128)(4,1)}, u32[]{:S(2)}) copy-start(pred[8]{0:T(512)(128)(4,1)} %iota_compare_fusion.5) | copy-start | bytes 28
  277.5 39.0 %copy-start.13 = (pred[8]{0:T(512)(128)(4,1)S(1)}, pred[8]{0:T(512)(128)(4,1)}, u32[]{:S(2)}) copy-start(pred[8]{0:T(512)(128)(4,1)} %iota_compare_fusion.6) | copy-start | bytes 28
  277.5 39.0 %copy-start.14 = (pred[8]{0:T(512)(128)(4,1)S(1)}, pred[8]{0:T(512)(128)(4,1)}, u32[]{:S(2)}) copy-start(pred[8]{0:T(512)(128)(4,1)} %iota_compare_fusion.7) | copy-start | bytes 28
  277.5 39.0 %copy-start.15 = (pred[8]{0:T(512)(128)(4,1)S(1)}, pred[8]{0:T(512)(128)(4,1)}, u32[]{:S(2)}) copy-start(pred[8]{0:T(512)(128)(4,1)} %iota_compare_fusion.8) | copy-start | bytes 28
  277.5 39.2 %copy-start.17 = (f32[8,160]{1,0:T(8,128)S(1)}, f32[8,160]{1,0:T(8,128)}, u32[]{:S(2)}) copy-start(f32[8,160]{1,0:T(8,128)} %param.14) | copy-start | bytes 15364
  277.5 39.1 %copy-start.19 = (s32[160]{0:T(256)S(1)}, s32[160]{0:T(256)}, u32[]{:S(2)}) copy-start(s32[160]{0:T(256)} %iota_add_fusion) | copy-start | bytes 1924
  277.5 40.0 %copy-start.1 = (bf16[8192,128]{1,0:T(8,128)(2,1)S(1)}, bf16[8192,128]{1,0:T(8,128)(2,1)}, u32[]{:S(2)}) copy-start(bf16[8192,128]{1,0:T(8,128)(2,1)} %param.22) | copy-start | bytes 6291460
  299.8 12.9 %collective-permute-start.13 = (f32[160]{0:T(256)S(1)}, f32[160]{0:T(256)S(1)}, u32[]{:S(2)}, u32[]{:S(2)}) collective-permute-start(f32[160]{0:T(256)S(1)} %get-tuple-element.52), channel_id=1, source_target_pairs={{0,124},{4,0},{8,4},{12,8},{16,12},{20,16},{24,20},{28,24},{32,28}... | collective-permute-start | bytes 1928 | tf_op jit(solution)/shard_map/ppermute | solution.py:16
  302.7 10.4 %collective-permute-start.12 = (f32[160]{0:T(256)S(1)}, f32[160]{0:T(256)S(1)}, u32[]{:S(2)}, u32[]{:S(2)}) collective-permute-start(f32[160]{0:T(256)S(1)} %get-tuple-element.51), channel_id=1, source_target_pairs={{0,120},{4,124},{8,0},{12,4},{16,8},{20,12},{24,16},{28,20},{32,24... | collective-permute-start | bytes 1928 | tf_op jit(solution)/shard_map/ppermute | solution.py:16
  308.3 6.3 %collective-permute-start.11 = (f32[160]{0:T(256)S(1)}, f32[160]{0:T(256)S(1)}, u32[]{:S(2)}, u32[]{:S(2)}) collective-permute-start(f32[160]{0:T(256)S(1)} %get-tuple-element.50), channel_id=1, source_target_pairs={{0,116},{4,120},{8,124},{12,0},{16,4},{20,8},{24,12},{28,16},{32,2... | collective-permute-start | bytes 1928 | tf_op jit(solution)/shard_map/ppermute | solution.py:16
  309.2 5.4 %collective-permute-start.10 = (f32[160]{0:T(256)S(1)}, f32[160]{0:T(256)S(1)}, u32[]{:S(2)}, u32[]{:S(2)}) collective-permute-start(f32[160]{0:T(256)S(1)} %get-tuple-element.49), channel_id=1, source_target_pairs={{0,112},{4,116},{8,120},{12,124},{16,0},{20,4},{24,8},{28,12},{32,... | collective-permute-start | bytes 1928 | tf_op jit(solution)/shard_map/ppermute | solution.py:16
  309.5 5.1 %collective-permute-start.9 = (f32[160]{0:T(256)S(1)}, f32[160]{0:T(256)S(1)}, u32[]{:S(2)}, u32[]{:S(2)}) collective-permute-start(f32[160]{0:T(256)S(1)} %get-tuple-element.48), channel_id=1, source_target_pairs={{0,108},{4,112},{8,116},{12,120},{16,124},{20,0},{24,4},{28,8},{32... | collective-permute-start | bytes 1928 | tf_op jit(solution)/shard_map/ppermute | solution.py:16
  312.6 3.7 %collective-permute-start.8 = (f32[160]{0:T(256)S(1)}, f32[160]{0:T(256)S(1)}, u32[]{:S(2)}, u32[]{:S(2)}) collective-permute-start(f32[160]{0:T(256)S(1)} %get-tuple-element.47), channel_id=1, source_target_pairs={{0,104},{4,108},{8,112},{12,116},{16,120},{20,124},{24,0},{28,4},{... | collective-permute-start | bytes 1928 | tf_op jit(solution)/shard_map/ppermute | solution.py:16
  313.1 3.3 %collective-permute-start.7 = (f32[160]{0:T(256)S(1)}, f32[160]{0:T(256)S(1)}, u32[]{:S(2)}, u32[]{:S(2)}) collective-permute-start(f32[160]{0:T(256)S(1)} %get-tuple-element.46), channel_id=1, source_target_pairs={{0,100},{4,104},{8,108},{12,112},{16,116},{20,120},{24,124},{28,0}... | collective-permute-start | bytes 1928 | tf_op jit(solution)/shard_map/ppermute | solution.py:16
  316.6 0.9 copy-start.5
Sparse Core Ops, SparseCore 0:
  130.4 100.8 all-gather.1
where the time goes:
time: 325 us; the launch traced here: 324 us
  waiting for transfers between devices  149 us (46%)
  other arithmetic  42 us (13%)
  matrix products  41.8 us (13%)
  between operations  34.6 us (11%)
  starting transfers between devices  27 us (8%)
  local copies, waits for them, and re-layouts  22.7 us (7%)
  blocking collectives  7.21 us (2%)
    ppermute x14, waiting for transfers between devices, passed_along(): lax.ppermute(value, axis, [(i, (i + by) % length) for i in range(length)])  79.7 us
    all_gather x1, waiting for transfers between devices, local(): packed = lax.all_gather(own_part, 'mp', axis=1, tiled=True)  69.3 us
    ppermute x14, starting transfers between devices, passed_along(): lax.ppermute(value, axis, [(i, (i + by) % length) for i in range(length)])  27 us
    dot_general x1, matrix products, head_values(): jnp.einsum('hgqk,khd->qhgd', weights, value_rows, preferred_element_type=...  14.9 us
    dot_general x1, matrix products, local(): queries = jnp.dot(normed, w_query, preferred_element_type=jnp.float32)  14.8 us
    gather x1, local copies, waits for them, and re-layouts, local(): own_part = jnp.take(jnp.concatenate(received, axis=0), pick_rows, axis=0)  10.1 us
    eq x8, other arithmetic, local(): slot_lanes == slot_for(shift_by)  8.29 us
    reduce_sum x1, other arithmetic, head_values(): row_total = jnp.sum(exp_scores, axis=-1, keepdims=True)  7.83 us
  transfers between devices with their start and end apart: 15, of which 9 were waited for; matrix products, arithmetic and copies ran while one was open for 7% of the time, Pallas kernels for 0%

commit v1 on v0

--- a/solution.py
+++ b/solution.py
@@ -101,7 +101,11 @@
     values_out = jnp.dot(normed, w_value, preferred_element_type=jnp.float32)
     value_terms = head_values(queries, keys_out, values_out, segment_ids, positions, folded_head)
     value_terms = value_terms + jnp.sum(own_part.astype(jnp.float32) * value_head[None, :], axis=1)
-    packed_values = lax.psum(value_terms, "mp")
+    packed_values = value_terms
+    for hop in (1, 2):
+        packed_values = packed_values + lax.ppermute(
+            packed_values, "mp", [(dev, dev ^ hop) for dev in range(4)]
+        )
     padded = jnp.concatenate([packed_values, jnp.zeros((slot_rows,), jnp.float32)])
     slot_values = jnp.zeros((rollouts, slot_rows), jnp.float32)
     for shift_by in range(rollouts):

time: 325 us -> 338 us (1.040)
  waiting for transfers between devices: 149 us -> 167 us
  blocking collectives: 7.21 us -> 0 us
    all_gather x1, waiting for transfers between devices: 69.3 us -> 86.6 us  [local(): packed = lax.all_gather(own_part, 'mp', axis=1, tiled=True)]
    psum x1 -> x0, blocking collectives: 7.21 us -> none  [local(): packed_values = lax.psum(value_terms, 'mp')]
    ppermute x0 -> x2, starting transfers between devices: none -> 3.72 us  [local(): lax.ppermute(packed_values, 'mp', [(dev, dev ^ hop) for dev in range(4)])]
    unnamed x47 -> x43, local copies, waits for them, and re-layouts: 6.86 us -> 6.85 us
  transfers between devices with their start and end apart: 15 -> 17, of which waited for: 9 -> 10; matrix products, arithmetic and copies ran while one was open for 7% -> 7% of each run, Pallas kernels for 0% -> 0%
where the time goes in v1:
time: 338 us; the launch traced here: 337 us
  waiting for transfers between devices  167 us (49%)
  matrix products  41.8 us (12%)
  other arithmetic  41 us (12%)
  between operations  34.8 us (10%)
  starting transfers between devices  29.9 us (9%)
  local copies, waits for them, and re-layouts  22.7 us (7%)
    all_gather x1, waiting for transfers between devices, local(): packed = lax.all_gather(own_part, 'mp', axis=1, tiled=True)  86.6 us
    ppermute x14, waiting for transfers between devices, passed_along(): lax.ppermute(value, axis, [(i, (i + by) % length) for i in range(length)])  79.8 us
    ppermute x14, starting transfers between devices, passed_along(): lax.ppermute(value, axis, [(i, (i + by) % length) for i in range(length)])  26.1 us
    dot_general x1, matrix products, head_values(): jnp.einsum('hgqk,khd->qhgd', weights, value_rows, preferred_element_type=...  14.9 us
    dot_general x1, matrix products, local(): queries = jnp.dot(normed, w_query, preferred_element_type=jnp.float32)  14.8 us
    gather x1, local copies, waits for them, and re-layouts, local(): own_part = jnp.take(jnp.concatenate(received, axis=0), pick_rows, axis=0)  10.1 us
    reduce_sum x1, other arithmetic, head_values(): row_total = jnp.sum(exp_scores, axis=-1, keepdims=True)  7.83 us
    eq x8, other arithmetic, local(): slot_lanes == slot_for(shift_by)  7.19 us
  transfers between devices with their start and end apart: 17, of which 10 were waited for; matrix products, arithmetic and copies ran while one was open for 7% of the time, Pallas kernels for 0%

profile of v1, /device:TPU:1, one launch (start us, length us, event | category | flops | bytes accessed | tf_op | source)
XLA Modules:
  0.0 337.1 jit_solution(8515653503310208259)
XLA Ops:
  7.4 1.9 fusion.49
  14.4 3.8 %constant_dynamic-slice_fusion = (bf16[160,2048]{1,0:T(8,128)(2,1)S(1)}, bf16[160,2048]{1,0:T(8,128)(2,1)S(1)}, bf16[160,2048]{1,0:T(8,128)(2,1)S(1)}, bf16[160,...) fusion(bf16[1280,2048]{1,0:T(8,128)(2,1)} %param.13, ...), kind=kLoop, calls=%fused_computation.98 | loop fusion | bytes 10485792 | tf_op jit(solution)/shard_map/dynamic_slice | solution.py:83
  18.2 2.6 collective-permute-start
  20.8 1.2 collective-permute-start.1
  22.0 1.5 collective-permute-start.2
  23.6 1.9 collective-permute-start.3
  25.4 3.4 %collective-permute-start.4 = (bf16[160,2048]{1,0:T(8,128)(2,1)S(1)}, bf16[160,2048]{1,0:T(8,128)(2,1)S(1)}, u32[]{:S(2)}, u32[]{:S(2)}) collective-permute-start(bf16[160,2048]{1,0:T(8,128)(2,1)S(1)} %get-tuple-element.33), channel_id=1, source_target_pairs={{0,20},{4,24},{8,28},{12,32},{16,36},{20,40},{24,44},{28,48},{32,5... | collective-permute-start | bytes 1966088 | tf_op jit(solution)/shard_map/ppermute | solution.py:16
  29.0 5.8 %collective-permute-done = bf16[160,2048]{1,0:T(8,128)(2,1)S(1)} collective-permute-done((bf16[160,2048]{1,0:T(8,128)(2,1)S(1)}, bf16[160,2048]{1,0:T(8,128)(2,1)S(1)}, u32[]{:S(2)}, u32[]{:S(2)}) %collective-permute-start) | collective-permute-done | bytes 655392 | tf_op jit(solution)/shard_map/ppermute | solution.py:16
  34.8 2.8 collective-permute-start.5
  37.6 0.9 constant_dynamic-update-slice_fusion.6
  38.5 14.7 %collective-permute-done.1 = bf16[160,2048]{1,0:T(8,128)(2,1)S(1)} collective-permute-done((bf16[160,2048]{1,0:T(8,128)(2,1)S(1)}, bf16[160,2048]{1,0:T(8,128)(2,1)S(1)}, u32[]{:S(2)}, u32[]{:S(2)}) %collective-permute-start.1) | collective-permute-done | bytes 655392 | tf_op jit(solution)/shard_map/ppermute | solution.py:16
  53.2 0.9 constant_dynamic-update-slice_fusion.5
  54.1 8.8 %collective-permute-done.2 = bf16[160,2048]{1,0:T(8,128)(2,1)S(1)} collective-permute-done((bf16[160,2048]{1,0:T(8,128)(2,1)S(1)}, bf16[160,2048]{1,0:T(8,128)(2,1)S(1)}, u32[]{:S(2)}, u32[]{:S(2)}) %collective-permute-start.2) | collective-permute-done | bytes 655392 | tf_op jit(solution)/shard_map/ppermute | solution.py:16
  62.9 0.9 constant_dynamic-update-slice_fusion.4
  63.8 35.7 %collective-permute-done.3 = bf16[160,2048]{1,0:T(8,128)(2,1)S(1)} collective-permute-done((bf16[160,2048]{1,0:T(8,128)(2,1)S(1)}, bf16[160,2048]{1,0:T(8,128)(2,1)S(1)}, u32[]{:S(2)}, u32[]{:S(2)}) %collective-permute-start.3) | collective-permute-done | bytes 655392 | tf_op jit(solution)/shard_map/ppermute | solution.py:16
  99.5 0.9 constant_dynamic-update-slice_fusion.3
  100.4 0.9 constant_dynamic-update-slice_fusion.2
  101.3 7.6 %collective-permute-done.5 = bf16[160,2048]{1,0:T(8,128)(2,1)S(1)} collective-permute-done((bf16[160,2048]{1,0:T(8,128)(2,1)S(1)}, bf16[160,2048]{1,0:T(8,128)(2,1)S(1)}, u32[]{:S(2)}, u32[]{:S(2)}) %collective-permute-start.5) | collective-permute-done | bytes 655392 | tf_op jit(solution)/shard_map/ppermute | solution.py:16
  108.9 0.9 constant_dynamic-update-slice_fusion.1
  109.8 5.4 %collective-permute-done.6 = bf16[160,2048]{1,0:T(8,128)(2,1)S(1)} collective-permute-done((bf16[160,2048]{1,0:T(8,128)(2,1)S(1)}, bf16[160,2048]{1,0:T(8,128)(2,1)S(1)}, u32[]{:S(2)}, u32[]{:S(2)}) %collective-permute-start.6) | collective-permute-done | bytes 655392 | tf_op jit(solution)/shard_map/ppermute | solution.py:16
  115.2 0.9 constant_dynamic-update-slice_fusion
  116.1 10.1 %gather_fusion = bf16[640,2048]{1,0:T(8,128)(2,1)} fusion(bf16[1280,2048]{1,0:T(8,128)(2,1)} %constant_dynamic-update-slice_fusion, s32[1024]{0:T(1024)S(1)} %pad_clamp_fusion), kind=kCustom, calls=%fused_computation | custom fusion | bytes 5245440 | tf_op jit(solution)/shard_map/jit(_take)/gather | solution.py:94
  126.2 4.1 %multiply_reduce_fusion = (f32[640]{0:T(1024)S(1)}, bf16[640,2048]{1,0:T(8,128)(2,1)}) fusion(f32[2048]{0:T(1024)S(1)} %copy-done.6, bf16[640,2048]{1,0:T(8,128)(2,1)} %gather_fusion, pred[640]{0:T(1024)(128)(4,1)S(1)} %compare_and_fusion.1), kind=kLoop, calls=%fused_computation.13 | loop fusion | flops 5242240 | bytes 5254272 | tf_op jit(solution)/shard_map/reduce_sum | solution.py:103
  130.3 1.2 iota_compare_fusion.3
  131.5 1.2 iota_compare_fusion.4
  132.7 1.1 iota_compare_fusion.5
  133.8 1.2 iota_compare_fusion.6
  135.5 5.9 %fusion.58 = (s32[]{:T(128)}, s32[]{:T(128)}, s32[]{:T(128)}, s32[]{:T(128)}, s32[]{:T(128)}, /*index=5*/s32[]{:T(128)}, s32[]{:T(128)}, s32[]{:T(128)}) fusion(s32[8]{0:T(128)S(1)} %copy-done.7, s32[]{:T(128)} %get-tuple-element.67, s32[]{:T(128)} %get-tuple-element.66, s32[]{:T(128)} %get-tuple-element.65, s32[]{:T(128)} %get-tuple-element.64, ...), kind=kLoop, calls=%fused_computation.140 | loop fusion | flops 184 | bytes 96 | tf_op jit(solution)/shard_map/reduce_sum | solution.py:114
  141.4 1.1 compare_and_fusion
  142.6 2.0 multiply_cosine_fusion
  144.6 86.6 %all-gather.2.cloned.1.call-done = bf16[640,8192]{1,0:T(8,128)(2,1)} async-done(((bf16[640,2048]{1,0:T(8,128)(2,1)}), bf16[640,8192]{1,0:T(8,128)(2,1)}) %all-gather.2.cloned.1.call-update) | async-done | bytes 10485776 | tf_op jit(solution)/shard_map/all_gather | solution.py:95
  231.3 6.2 %fusion = f32[640]{0:T(1024)S(1)} fusion(bf16[640,8192]{1,0:T(8,128)(2,1)} %all-gather.2.cloned.1.call-done), kind=kLoop, calls=%fused_computation.3 | loop fusion | flops 15728000 | bytes 10488320 | tf_op jit(solution)/shard_map/reduce_sum | solution.py:97
  238.2 14.8 %convolution_bitcast_fusion = f32[80,8,8,128]{3,1,2,0:T(8,128)S(1)} fusion(bf16[8192,1024]{1,0:T(8,128)(2,1)} %param.21, bf16[640,8192]{1,0:T(8,128)(2,1)S(1)} %copy-done.2, f32[8192]{0:T(1024)} %param.20, f32[640]{0:T(1024)S(1)} %add_rsqrt_fusion), kind=kOutput, calls=%fused_computation.19 | convolution fusion | flops 10758389760 | bytes 29919744 | tf_op jit(solution)/shard_map/dot_general | solution.py:99
  254.5 4.9 %convolution_bitcast_fusion.1 = f32[640,1,128]{0,2,1:T(8,128)} fusion(bf16[8192,128]{1,0:T(8,128)(2,1)S(1)} %copy-done, bf16[640,8192]{1,0:T(8,128)(2,1)S(1)} %copy-done.2, f32[8192]{0:T(1024)} %param.20, f32[640]{0:T(1024)S(1)} %add_rsqrt_fusion), kind=kOutput, calls=%fused_computation.25 | convolution fusion | flops 1363148800 | bytes 12945920 | tf_op jit(solution)/shard_map/dot_general | solution.py:100
  259.4 1.7 fusion.36
  261.1 2.1 subtract_convert_fusion
  263.2 6.4 %fusion.3 = (f32[8,640]{1,0:T(8,128)S(1)}, f32[640,640,8]{1,0,2:T(8,128)}) fusion(pred[640,640]{0,1:T(8,128)(4,1)S(1)} %copy-done.3, bf16[640,8,64]{2,0,1:T(8,128)(2,1)S(1)} %get-tuple-element.31, bf16[640,8,64]{2,0,1:T(8,128)(2,1)S(1)} %get-tuple-element.30, bf16[640,64]{0,1:T(8,128)(2,1)S(1)} %get-tuple-element.43, bf16[640,64]{0,1:T(8,128)(2,1)S(1)} %get-tuple-element.42), kind=kOutput, calls=%fused_computation.9 | convolution fusion | flops 851635200 | bytes 15011840 | tf_op jit(solution)/shard_map/qhgd,khd->hgqk/dot_general | solution.py:43
  269.6 7.8 %fusion.4 = f32[8,640]{1,0:T(8,128)S(1)} fusion(f32[640,640,8]{1,0,2:T(8,128)} %get-tuple-element.58, f32[8,640]{1,0:T(8,128)S(1)} %get-tuple-element.57, pred[640,640]{0,1:T(8,128)(4,1)S(1)} %copy-done.3), kind=kLoop, calls=%fused_computation.10 | loop fusion | flops 16378880 | bytes 13557760 | tf_op jit(solution)/shard_map/reduce_sum | solution.py:50
  277.6 14.9 %fusion.7 = f32[640]{0:T(1024)S(1)} fusion(f32[8,640]{1,0:T(8,128)S(1)} %fusion.4, f32[8,640]{1,0:T(8,128)S(1)} %get-tuple-element.57, f32[640,640,8]{1,0,2:T(8,128)} %get-tuple-element.58, pred[640,640]{0,1:T(8,128)(4,1)S(1)} %copy-done.3, f32[8,128]{1,0:T(8,128)S(1)} %bitcast.51, bf16[8192,128]{1,0:T(8,128)(2,1)} %param.23, ...), kind=kOutput, calls=%fused_computation.15 | convolution fusion | flops 2223062528 | bytes 26182656 | tf_op jit(solution)/shard_map/hgqk,khd->qhgd/dot_general | solution.py:52
  292.5 1.3 collective-permute-start.7
  295.0 2.4 collective-permute-start.8
  313.4 2.3 collective-permute-start.15
  315.7 4.8 %collective-permute-start.14 = (f32[160]{0:T(256)S(1)}, f32[160]{0:T(256)S(1)}, u32[]{:S(2)}, u32[]{:S(2)}) collective-permute-start(f32[160]{0:T(256)S(1)} %get-tuple-element.51), channel_id=1, source_target_pairs={{0,120},{4,124},{8,0},{12,4},{16,8},{20,12},{24,16},{28,20},{32,24... | collective-permute-start | bytes 1928 | tf_op jit(solution)/shard_map/ppermute | solution.py:16
  321.0 0.9 collective-permute-start.13
  321.9 0.9 collective-permute-start.12
  322.8 2.6 collective-permute-start.11
  327.3 1.7 collective-permute-done.10
  329.4 0.8 fusion.25
  (71 shorter events, 7.8 us)
Async XLA Ops:
  7.2 247.3 %copy-start = (bf16[8192,128]{1,0:T(8,128)(2,1)S(1)}, bf16[8192,128]{1,0:T(8,128)(2,1)}, u32[]{:S(2)}) copy-start(bf16[8192,128]{1,0:T(8,128)(2,1)} %param.22) | copy-start | bytes 6291460
  7.2 224.1 %all-gather.2.cloned.1.call-start = ((), (), s32[]{:S(2)}) async-start(), calls=%async_computation | async-start | bytes 13107200 | tf_op jit(solution)/shard_map/all_gather | solution.py:95
  14.4 14.4 %copy-start.4 = (s32[640]{0:T(1024)S(1)}, s32[640]{0:T(1024)}, u32[]{:S(2)}) copy-start(s32[640]{0:T(1024)} %param.19) | copy-start | bytes 7684
  14.4 14.4 %copy-start.7 = (s32[8]{0:T(128)S(1)}, s32[8]{0:T(128)}, u32[]{:S(2)}) copy-start(s32[8]{0:T(128)} %param.18) | copy-start | bytes 100
  18.2 16.6 %collective-permute-start = (bf16[160,2048]{1,0:T(8,128)(2,1)S(1)}, bf16[160,2048]{1,0:T(8,128)(2,1)S(1)}, u32[]{:S(2)}, u32[]{:S(2)}) collective-permute-start(bf16[160,2048]{1,0:T(8,128)(2,1)S(1)} %get-tuple-element.37), channel_id=1, source_target_pairs={{0,4},{4,8},{8,12},{12,16},{16,20},{20,24},{24,28},{28,32},{32,36}... | collective-permute-start | bytes 1966088 | tf_op jit(solution)/shard_map/ppermute | solution.py:16
  20.8 32.4 %collective-permute-start.1 = (bf16[160,2048]{1,0:T(8,128)(2,1)S(1)}, bf16[160,2048]{1,0:T(8,128)(2,1)S(1)}, u32[]{:S(2)}, u32[]{:S(2)}) collective-permute-start(bf16[160,2048]{1,0:T(8,128)(2,1)S(1)} %get-tuple-element.36), channel_id=1, source_target_pairs={{0,8},{4,12},{8,16},{12,20},{16,24},{20,28},{24,32},{28,36},{32,40... | collective-permute-start | bytes 1966088 | tf_op jit(solution)/shard_map/ppermute | solution.py:16
  22.0 40.8 %collective-permute-start.2 = (bf16[160,2048]{1,0:T(8,128)(2,1)S(1)}, bf16[160,2048]{1,0:T(8,128)(2,1)S(1)}, u32[]{:S(2)}, u32[]{:S(2)}) collective-permute-start(bf16[160,2048]{1,0:T(8,128)(2,1)S(1)} %get-tuple-element.35), channel_id=1, source_target_pairs={{0,12},{4,16},{8,20},{12,24},{16,28},{20,32},{24,36},{28,40},{32,4... | collective-permute-start | bytes 1966088 | tf_op jit(solution)/shard_map/ppermute | solution.py:16
  23.6 75.9 %collective-permute-start.3 = (bf16[160,2048]{1,0:T(8,128)(2,1)S(1)}, bf16[160,2048]{1,0:T(8,128)(2,1)S(1)}, u32[]{:S(2)}, u32[]{:S(2)}) collective-permute-start(bf16[160,2048]{1,0:T(8,128)(2,1)S(1)} %get-tuple-element.34), channel_id=1, source_target_pairs={{0,16},{4,20},{8,24},{12,28},{16,32},{20,36},{24,40},{28,44},{32,4... | collective-permute-start | bytes 1966088 | tf_op jit(solution)/shard_map/ppermute | solution.py:16
  25.4 75.0 %collective-permute-start.4 = (bf16[160,2048]{1,0:T(8,128)(2,1)S(1)}, bf16[160,2048]{1,0:T(8,128)(2,1)S(1)}, u32[]{:S(2)}, u32[]{:S(2)}) collective-permute-start(bf16[160,2048]{1,0:T(8,128)(2,1)S(1)} %get-tuple-element.33), channel_id=1, source_target_pairs={{0,20},{4,24},{8,28},{12,32},{16,36},{20,40},{24,44},{28,48},{32,5... | collective-permute-start | bytes 1966088 | tf_op jit(solution)/shard_map/ppermute | solution.py:16
  34.8 74.1 %collective-permute-start.5 = (bf16[160,2048]{1,0:T(8,128)(2,1)S(1)}, bf16[160,2048]{1,0:T(8,128)(2,1)S(1)}, u32[]{:S(2)}, u32[]{:S(2)}) collective-permute-start(bf16[160,2048]{1,0:T(8,128)(2,1)S(1)} %get-tuple-element.39), channel_id=1, source_target_pairs={{0,24},{4,28},{8,32},{12,36},{16,40},{20,44},{24,48},{28,52},{32,5... | collective-permute-start | bytes 1966088 | tf_op jit(solution)/shard_map/ppermute | solution.py:16
  53.2 62.0 %collective-permute-start.6 = (bf16[160,2048]{1,0:T(8,128)(2,1)S(1)}, bf16[160,2048]{1,0:T(8,128)(2,1)S(1)}, u32[]{:S(2)}, u32[]{:S(2)}) collective-permute-start(bf16[160,2048]{1,0:T(8,128)(2,1)S(1)} %get-tuple-element.32), channel_id=1, source_target_pairs={{0,28},{4,32},{8,36},{12,40},{16,44},{20,48},{24,52},{28,56},{32,6... | collective-permute-start | bytes 1966088 | tf_op jit(solution)/shard_map/ppermute | solution.py:16
  116.1 10.1 %copy-start.6 = (f32[2048]{0:T(1024)S(1)}, f32[2048]{0:T(1024)}, u32[]{:S(2)}) copy-start(f32[2048]{0:T(1024)} %param.24) | copy-start | bytes 24580
  130.3 14.3 %copy-start.8 = (f32[64]{0:T(128)}, f32[64]{0:T(128)S(1)}, u32[]{:S(2)}) copy-start(f32[64]{0:T(128)S(1)} %multiply_power_fusion) | copy-start | bytes 772
  231.3 7.0 %copy-start.2 = (bf16[640,8192]{1,0:T(8,128)(2,1)S(1)}, bf16[640,8192]{1,0:T(8,128)(2,1)}, u32[]{:S(2)}) copy-start(bf16[640,8192]{1,0:T(8,128)(2,1)} %all-gather.2.cloned.1.call-done) | copy-start | bytes 31457284
  259.4 3.8 %copy-start.3 = (pred[640,640]{0,1:T(8,128)(4,1)S(1)}, pred[640,640]{0,1:T(8,128)(4,1)}, u32[]{:S(2)}) copy-start(pred[640,640]{0,1:T(8,128)(4,1)} %compare_and_fusion) | copy-start | bytes 1228804
  269.6 7.8 %copy-start.14 = (f32[8192]{0:T(1024)S(1)}, f32[8192]{0:T(1024)}, u32[]{:S(2)}) copy-start(f32[8192]{0:T(1024)} %param.20) | copy-start | bytes 98308
  269.6 7.8 %copy-start.16 = (f32[1024]{0:T(1024)S(1)}, f32[1024]{0:T(1024)}, u32[]{:S(2)}) copy-start(f32[1024]{0:T(1024)} %param.25) | copy-start | bytes 12292
  277.5 51.7 %copy-start.9 = (s32[8]{0:T(128)S(1)}, s32[8]{0:T(128)}, u32[]{:S(2)}) copy-start(s32[8]{0:T(128)} %param.15) | copy-start | bytes 100
  277.5 51.7 %copy-start.10 = (pred[8]{0:T(512)(128)(4,1)S(1)}, pred[8]{0:T(512)(128)(4,1)}, u32[]{:S(2)}) copy-start(pred[8]{0:T(512)(128)(4,1)} %iota_compare_fusion.3) | copy-start | bytes 28
  277.5 51.7 %copy-start.11 = (pred[8]{0:T(512)(128)(4,1)S(1)}, pred[8]{0:T(512)(128)(4,1)}, u32[]{:S(2)}) copy-start(pred[8]{0:T(512)(128)(4,1)} %iota_compare_fusion.4) | copy-start | bytes 28
  277.5 51.7 %copy-start.12 = (pred[8]{0:T(512)(128)(4,1)S(1)}, pred[8]{0:T(512)(128)(4,1)}, u32[]{:S(2)}) copy-start(pred[8]{0:T(512)(128)(4,1)} %iota_compare_fusion.5) | copy-start | bytes 28
  277.5 51.7 %copy-start.13 = (pred[8]{0:T(512)(128)(4,1)S(1)}, pred[8]{0:T(512)(128)(4,1)}, u32[]{:S(2)}) copy-start(pred[8]{0:T(512)(128)(4,1)} %iota_compare_fusion.6) | copy-start | bytes 28
  277.5 51.9 %copy-start.15 = (f32[8,160]{1,0:T(8,128)S(1)}, f32[8,160]{1,0:T(8,128)}, u32[]{:S(2)}) copy-start(f32[8,160]{1,0:T(8,128)} %param.14) | copy-start | bytes 15364
  277.5 51.8 %copy-start.17 = (s32[160]{0:T(256)S(1)}, s32[160]{0:T(256)}, u32[]{:S(2)}) copy-start(s32[160]{0:T(256)} %iota_add_fusion) | copy-start | bytes 1924
  277.6 52.7 %copy-start.1 = (bf16[8192,128]{1,0:T(8,128)(2,1)S(1)}, bf16[8192,128]{1,0:T(8,128)(2,1)}, u32[]{:S(2)}) copy-start(bf16[8192,128]{1,0:T(8,128)(2,1)} %param.22) | copy-start | bytes 6291460
  292.5 2.5 collective-permute-start.7
  295.0 18.2 %collective-permute-start.8 = (f32[640]{0:T(1024)S(1)}, f32[640]{0:T(1024)S(1)}, u32[]{:S(2)}, u32[]{:S(2)}) collective-permute-start(f32[640]{0:T(1024)S(1)} %add.257), channel_id=1, source_target_pairs={{0,2},{1,3},{2,0},{3,1},{4,6},{5,7},{6,4},{7,5},{8,10},{9,11},{10,... | collective-permute-start | bytes 7688 | tf_op jit(solution)/shard_map/ppermute | solution.py:106
  313.4 12.0 %collective-permute-start.15 = (f32[160]{0:T(256)S(1)}, f32[160]{0:T(256)S(1)}, u32[]{:S(2)}, u32[]{:S(2)}) collective-permute-start(f32[160]{0:T(256)S(1)} %get-tuple-element.52), channel_id=1, source_target_pairs={{0,124},{4,0},{8,4},{12,8},{16,12},{20,16},{24,20},{28,24},{32,28}... | collective-permute-start | bytes 1928 | tf_op jit(solution)/shard_map/ppermute | solution.py:16
  315.7 10.2 %collective-permute-start.14 = (f32[160]{0:T(256)S(1)}, f32[160]{0:T(256)S(1)}, u32[]{:S(2)}, u32[]{:S(2)}) collective-permute-start(f32[160]{0:T(256)S(1)} %get-tuple-element.51), channel_id=1, source_target_pairs={{0,120},{4,124},{8,0},{12,4},{16,8},{20,12},{24,16},{28,20},{32,24... | collective-permute-start | bytes 1928 | tf_op jit(solution)/shard_map/ppermute | solution.py:16
  321.0 6.3 %collective-permute-start.13 = (f32[160]{0:T(256)S(1)}, f32[160]{0:T(256)S(1)}, u32[]{:S(2)}, u32[]{:S(2)}) collective-permute-start(f32[160]{0:T(256)S(1)} %get-tuple-element.50), channel_id=1, source_target_pairs={{0,116},{4,120},{8,124},{12,0},{16,4},{20,8},{24,12},{28,16},{32,2... | collective-permute-start | bytes 1928 | tf_op jit(solution)/shard_map/ppermute | solution.py:16
  321.9 5.4 %collective-permute-start.12 = (f32[160]{0:T(256)S(1)}, f32[160]{0:T(256)S(1)}, u32[]{:S(2)}, u32[]{:S(2)}) collective-permute-start(f32[160]{0:T(256)S(1)} %get-tuple-element.49), channel_id=1, source_target_pairs={{0,112},{4,116},{8,120},{12,124},{16,0},{20,4},{24,8},{28,12},{32,... | collective-permute-start | bytes 1928 | tf_op jit(solution)/shard_map/ppermute | solution.py:16
  322.8 4.5 %collective-permute-start.11 = (f32[160]{0:T(256)S(1)}, f32[160]{0:T(256)S(1)}, u32[]{:S(2)}, u32[]{:S(2)}) collective-permute-start(f32[160]{0:T(256)S(1)} %get-tuple-element.48), channel_id=1, source_target_pairs={{0,108},{4,112},{8,116},{12,120},{16,124},{20,0},{24,4},{28,8},{32... | collective-permute-start | bytes 1928 | tf_op jit(solution)/shard_map/ppermute | solution.py:16
  325.4 3.7 %collective-permute-start.10 = (f32[160]{0:T(256)S(1)}, f32[160]{0:T(256)S(1)}, u32[]{:S(2)}, u32[]{:S(2)}) collective-permute-start(f32[160]{0:T(256)S(1)} %get-tuple-element.47), channel_id=1, source_target_pairs={{0,104},{4,108},{8,112},{12,116},{16,120},{20,124},{24,0},{28,4},{... | collective-permute-start | bytes 1928 | tf_op jit(solution)/shard_map/ppermute | solution.py:16
  325.9 3.3 collective-permute-start.9
  329.3 0.9 copy-start.5
Sparse Core Ops, SparseCore 0:
  130.4 100.8 all-gather.1
